TPU v7x, 32 devices: a whole 2x2x4 slice. The times are simulated.
32 devices in a mesh: ctx: 4 (over y, x), exp: 8 (over z, core).
Axes of the slice: x: 2, y: 2, z: 4, core: 2. Of those that a mesh axis runs over, the one named last changes fastest.
Arguments:
- queries: bfloat16 [512, 12288], P('ctx', 'exp'), may hold values from -40.35234 to 40.35234
- key_rows: bfloat16 [512, 12288], P('ctx', 'exp'), may hold values from -4 to 4
- value_rows: bfloat16 [512, 8192], P('ctx', 'exp'), may hold values from -6 to 6
- w_out: bfloat16 [8192, 3584], P('exp'), may hold values from -0.5 to 0.5
- residual: bfloat16 [512, 3584], P(('ctx', 'exp')), may hold values from -3 to 3
- norm_gain: float32 [3584], replicated, may hold values from 0.1 to 1.9
- router: bfloat16 [3584, 32], replicated, may hold values from -0.09375 to 0.09375
- routing: int32 [8, 4, 16, 8], P('exp'), may hold values from 0 to 31, all different within a row; in each aligned block of 64 rows (0 to 63, 64 to 127, ..., all dimensions but the last counted through in order) at most 24 rows name the same one
- w_gate: bfloat16 [32, 3584, 2048], P('exp', None, 'ctx'), may hold values from -0.09375 to 0.09375
- w_up: bfloat16 [32, 3584, 2048], P('exp', None, 'ctx'), may hold values from -0.09375 to 0.09375
- w_down: bfloat16 [32, 2048, 3584], P('exp', 'ctx'), may hold values from -0.125 to 0.125
Outputs:
- mixed: bfloat16 [512, 3584], P(('ctx', 'exp'))
Inputs may be any that keep to these rules, and one draw needn't show every extreme that they name: `routing`: each token lists 8 different experts. Among the 64 tokens at one index of the first dimension, no expert is listed more than 24 times, and in every draw some expert is listed exactly 24 times in some such group.
All inputs are finite; a program needn't handle non-finite values.
Results may differ from a plain program's by a relative error of at most 0.025.
Values may be sent and summed in bfloat16 or wider, within the bound.
A program may use at most 128 MiB of HBM per device.

v0:
```python
import jax
import jax.numpy as jnp
from jax import lax
from jax.sharding import PartitionSpec as P

DQK = 192
DV = 128
NEG = -1e30


def from_behind(block, axis, distance):
    devices = range(lax.axis_size(axis))
    route = [((i - distance) % len(devices), i) for i in devices]
    return lax.ppermute(block, axis, route)


def body(
    queries, key_rows, value_rows, w_out, residual, norm_gain, router, routing, w_gate, w_up, w_down
):
    ctx_index = lax.axis_index("ctx")
    ctx_count = lax.axis_size("ctx")
    tok_rows = queries.shape[0]
    heads_here = queries.shape[1] // DQK
    q_full = queries.reshape(tok_rows, heads_here, DQK)
    k_full = key_rows.reshape(tok_rows, heads_here, DQK)
    v_full = value_rows.reshape(tok_rows, heads_here, DV)
    positions = jnp.arange(tok_rows, dtype=jnp.int32)
    score_scale = DQK ** (-0.5)

    def attend(state, q_part, k_part, v_part, q_source, k_source):
        row_max, row_total, accum = state
        scores = (
            jnp.einsum("thd,shd->hts", q_part, k_part, preferred_element_type=jnp.float32)
            * score_scale
        )
        query_pos = q_source * tok_rows + positions
        key_pos = k_source * tok_rows + positions
        allowed = (key_pos[None, :] <= query_pos[:, None])[None]
        scores = jnp.where(allowed, scores, NEG)
        new_max = jnp.maximum(row_max, jnp.max(scores, axis=-1))
        probs = jnp.where(allowed, jnp.exp(scores - new_max[..., None]), 0.0)
        carry_scale = jnp.exp(row_max - new_max)
        row_total = row_total * carry_scale + jnp.sum(probs, axis=-1)
        accum = accum * carry_scale[..., None] + jnp.einsum(
            "hts,shd->htd", probs, v_part.astype(jnp.float32), precision=lax.Precision.HIGHEST
        )
        return (new_max, row_total, accum)

    def visit(state, q_part, k_part, v_part, q_source, k_source):
        return attend(state, q_part, k_part, v_part, q_source, k_source)

    home = visit(
        (
            jnp.full((heads_here, tok_rows), NEG, jnp.float32),
            jnp.zeros((heads_here, tok_rows), jnp.float32),
            jnp.zeros((heads_here, tok_rows, DV), jnp.float32),
        ),
        q_full,
        k_full,
        v_full,
        ctx_index,
        ctx_index,
    )

    def turn(turn_index, carry):
        state, k_now, v_now = carry
        k_now, v_now = from_behind((k_now, v_now), "ctx", -1)
        source = (ctx_index + turn_index + 1) % ctx_count
        state = visit(state, q_full, k_now, v_now, ctx_index, source)
        return (state, k_now, v_now)

    carried = lax.fori_loop(0, ctx_count - 1, turn, (home, k_full, v_full))
    row_total, accum = (carried[0][1], carried[0][2])
    final = accum / row_total[..., None]
    attended = final.transpose(1, 0, 2).reshape(tok_rows, heads_here * DV).astype(jnp.bfloat16)
    attn_out = lax.psum_scatter(
        jnp.dot(attended, w_out, preferred_element_type=jnp.float32).astype(jnp.bfloat16),
        "exp",
        scatter_dimension=0,
        tiled=True,
    ).astype(jnp.float32)
    hidden_state = residual.astype(jnp.float32) + attn_out
    mean_square = jnp.mean(hidden_state * hidden_state, axis=-1, keepdims=True)
    normed = (hidden_state * lax.rsqrt(mean_square + 1e-06) * norm_gain).astype(jnp.bfloat16)
    column = lax.all_gather(normed, "ctx", axis=0, tiled=True)
    experts = router.shape[1]
    top_count = routing.shape[-1]
    routes = routing.reshape(-1, top_count)
    group_rows = routes.shape[0]
    capacity = 3 * group_rows * top_count // (2 * experts)
    d_model = column.shape[1]
    affinity = jax.nn.sigmoid(jnp.dot(column, router, preferred_element_type=jnp.float32))
    onehot = routes[:, :, None] == jnp.arange(experts, dtype=jnp.int32)[None, None, :]
    chosen = jnp.sum(jnp.where(onehot, affinity[:, None, :], 0.0), axis=-1)
    route_weight = 2.5 * chosen / jnp.sum(chosen, axis=-1, keepdims=True)
    flat_hot = onehot.reshape(group_rows * top_count, experts).astype(jnp.int32)
    before = jnp.cumsum(flat_hot, axis=0) - flat_hot
    slot_index = jnp.sum(before * flat_hot, axis=-1)
    target = routes.reshape(-1) * capacity + slot_index
    matches = (target[:, None] == jnp.arange(experts * capacity, dtype=jnp.int32)[None, :]).reshape(
        group_rows, top_count, experts * capacity
    )
    dispatch_table = jnp.any(matches, axis=1).T.astype(jnp.bfloat16)
    outgoing = jnp.dot(dispatch_table, column, preferred_element_type=jnp.float32).astype(
        jnp.bfloat16
    )
    outgoing = outgoing.reshape(experts, capacity, d_model)
    arrived = lax.all_to_all(outgoing, "exp", split_axis=0, concat_axis=0, tiled=True)
    local_experts = w_gate.shape[0]
    sources = arrived.shape[0] // local_experts
    slots_here = arrived.shape[1]
    inputs = arrived.reshape(sources, local_experts, slots_here, d_model)
    gate = jnp.einsum("sexd,edf->sexf", inputs, w_gate, preferred_element_type=jnp.float32)
    upper = jnp.einsum("sexd,edf->sexf", inputs, w_up, preferred_element_type=jnp.float32)
    expert_hidden = (jax.nn.silu(gate) * upper).astype(jnp.bfloat16)
    partial_value = jnp.einsum(
        "sexf,efd->sexd", expert_hidden, w_down, preferred_element_type=jnp.float32
    ).astype(jnp.bfloat16)
    partial_value = partial_value.reshape(sources * local_experts, slots_here, d_model)
    returned = lax.all_to_all(partial_value, "exp", split_axis=0, concat_axis=0, tiled=True)
    flat_back = returned.reshape(experts * capacity, d_model)
    picked = (
        jnp.take(flat_back, target, axis=0)
        .reshape(group_rows, top_count, d_model)
        .astype(jnp.float32)
    )
    combined = jnp.sum(picked * route_weight[..., None], axis=1)
    moe_out = lax.psum_scatter(
        combined.astype(jnp.bfloat16), "ctx", scatter_dimension=0, tiled=True
    ).astype(jnp.float32)
    return (hidden_state + moe_out).astype(jnp.bfloat16)


def solution(mesh):
    in_specs = (
        P("ctx", "exp"),
        P("ctx", "exp"),
        P("ctx", "exp"),
        P("exp", None),
        P(("ctx", "exp"), None),
        P(),
        P(),
        P("exp", None, None, None),
        P("exp", None, "ctx"),
        P("exp", None, "ctx"),
        P("exp", "ctx", None),
    )
    out_specs = P(("ctx", "exp"), None)
    return jax.shard_map(body, mesh=mesh, in_specs=in_specs, out_specs=out_specs, check_vma=False)
```

profile of v0, /device:TPU:0, one launch (start us, length us, event | category | flops | bytes accessed | tf_op | source)
XLA Modules:
  0.0 447.0 jit_solution(17789973888606974906)
XLA Ops:
  6.5 0.1 broadcast_compare_fusion.1
  6.6 1.1 copy.40
  7.8 0.2 copy.43
  8.0 1.2 copy.38
  9.2 1.2 copy.39
  10.4 0.4 fusion.46
  10.8 0.1 fusion.35
  10.9 0.6 convolution_add_fusion.1
  11.6 54.3 %while.25 = (s32[]{:T(128)}, f32[8,128]{1,0:T(8,128)S(1)}, f32[8,128]{1,0:T(8,128)S(1)}, f32[8,128,128]{2,1,0:T(8,128)S(1)}, bf16[128,8,192]{0,2,1:T(8,128)(2,1)...) while((s32[]{:T(128)}, f32[8,128]{1,0:T(8,128)S(1)}, ...), condition=%wide.region_5.6_spmd.clone.clone, body=%wide.region_2.5_spmd.clone.clone.sunk | while | flops 252987664 | bytes 7735662 | solution.py:72
  11.6 4.0 collective-permute-start
  15.6 0.5 collective-permute-start.1
  16.1 0.1 broadcast_compare_fusion.3
  16.2 13.4 %collective-permute-done.1 = bf16[128,8,128]{2,0,1:T(8,128)(2,1)S(1)} collective-permute-done((bf16[128,8,128]{2,0,1:T(8,128)(2,1)S(1)}, bf16[128,8,128]{2,0,1:T(8,128)(2,1)S(1)}, u32[]{:S(2)}, u32[]{:S(2)}) %collective-permute-start.1) | collective-permute-done | bytes 262176 | tf_op jit(solution)/shard_map/while/body/eval_jaxpr/ppermute | solution.py:14
  29.6 0.4 fusion.68
  30.0 0.1 fusion.69
  30.1 0.8 convolution_add_fusion.3
  30.9 3.4 collective-permute-start
  34.4 0.1 collective-permute-start.1
  34.4 0.1 broadcast_compare_fusion.3
  34.5 13.0 %collective-permute-done.1 = bf16[128,8,128]{2,0,1:T(8,128)(2,1)S(1)} collective-permute-done((bf16[128,8,128]{2,0,1:T(8,128)(2,1)S(1)}, bf16[128,8,128]{2,0,1:T(8,128)(2,1)S(1)}, u32[]{:S(2)}, u32[]{:S(2)}) %collective-permute-start.1) | collective-permute-done | bytes 262176 | tf_op jit(solution)/shard_map/while/body/eval_jaxpr/ppermute | solution.py:14
  47.5 0.4 fusion.68
  47.9 0.1 fusion.69
  48.1 0.8 convolution_add_fusion.3
  48.8 3.4 collective-permute-start
  52.3 0.1 collective-permute-start.1
  52.3 0.1 broadcast_compare_fusion.3
  52.4 12.1 %collective-permute-done.1 = bf16[128,8,128]{2,0,1:T(8,128)(2,1)S(1)} collective-permute-done((bf16[128,8,128]{2,0,1:T(8,128)(2,1)S(1)}, bf16[128,8,128]{2,0,1:T(8,128)(2,1)S(1)}, u32[]{:S(2)}, u32[]{:S(2)}) %collective-permute-start.1) | collective-permute-done | bytes 262176 | tf_op jit(solution)/shard_map/while/body/eval_jaxpr/ppermute | solution.py:14
  64.6 0.4 fusion.68
  65.0 0.1 fusion.69
  65.1 0.8 convolution_add_fusion.3
  65.9 0.2 copy.44
  66.2 5.2 %convolution_convert_fusion.1 = bf16[128,3584]{1,0:T(8,128)(2,1)} fusion(bf16[128,1024]{0,1:T(8,128)(2,1)S(1)} %bitcast.110, bf16[1024,3584]{1,0:T(8,128)(2,1)} %param.16), kind=kOutput, calls=%fused_computation.28 | convolution fusion | flops 939982848 | bytes 8519680 | tf_op jit(solution)/shard_map/dot_general | solution.py:77
  71.5 0.1 copy.46
  71.5 0.1 eq.55
  71.6 0.1 reshape_reshape.6
  71.7 0.1 reshape_reshape.5
  71.8 1.2 reduce-window.6
  73.0 0.2 slice_reduce_fusion
  73.2 0.1 fusion.41
  73.4 0.1 reduce_sum.76
  73.5 0.1 copy.51
  73.6 0.5 fusion.26
  74.2 31.8 %reduce-scatter.3.cloned.1.call-done = bf16[16,3584]{1,0:T(8,128)(2,1)} async-done(((bf16[128,3584]{1,0:T(8,128)(2,1)}), bf16[16,3584]{1,0:T(8,128)(2,1)}) %reduce-scatter.3.cloned.1.call-update) | async-done | bytes 114704 | tf_op jit(solution)/shard_map/reduce_scatter | solution.py:76
  106.0 1.0 multiply_reduce_fusion.1
  107.0 1.0 multiply_convert_fusion
  108.0 9.8 %all_gather.3 = bf16[64,3584]{1,0:T(8,128)(2,1)S(1)} all-gather(bf16[16,3584]{1,0:T(8,128)(2,1)S(1)} %multiply_convert_fusion), channel_id=1, replica_groups=mesh['ctx'=4,'exp'=8] {'ctx'}, dimensions={0}, use_global_device_ids=true | all-gather | bytes 573440 | tf_op jit(solution)/shard_map/all_gather | solution.py:85
  117.8 1.6 convolution_convert_fusion
  119.4 124.6 %all_to_all.10 = bf16[32,24,3584]{2,1,0:T(8,128)(2,1)S(1)} all-to-all(bf16[32,24,3584]{2,1,0:T(8,128)(2,1)S(1)} %bitcast.102), channel_id=1, replica_groups=mesh['ctx'=4,'exp'=8] {'exp'}, dimensions={0} | all-to-all | bytes 11010048 | tf_op jit(solution)/shard_map/all_to_all | solution.py:108
  244.0 6.9 %fusion.12 = f32[4,8,24,512]{3,2,1,0:T(8,128)S(1)} fusion(bf16[4,3584,512]{2,1,0:T(8,128)(2,1)} %param.21, bf16[8,4,24,3584]{3,2,1,0:T(8,128)(2,1)S(1)} %bitcast.106), kind=kOutput, calls=%fused_computation.20 | convolution fusion | flops 2818572288 | bytes 21757952 | tf_op jit(solution)/shard_map/sexd,edf->sexf/dot_general | solution.py:113
  250.9 8.6 %fusion.22 = bf16[8,4,24,512]{3,2,0,1:T(8,128)(2,1)S(1)} fusion(f32[4,8,24,512]{3,2,1,0:T(8,128)S(1)} %fusion.12, bf16[4,3584,512]{2,1,0:T(8,128)(2,1)} %param.22, bf16[8,4,24,3584]{3,2,1,0:T(8,128)(2,1)S(1)} %bitcast.107), kind=kOutput, calls=%fused_computation.31 | convolution fusion | flops 2820931584 | bytes 22544384 | tf_op jit(solution)/shard_map/sexd,edf->sexf/dot_general | solution.py:114
  259.5 8.2 %fusion.17 = bf16[8,4,24,3584]{3,2,0,1:T(8,128)(2,1)S(1)} fusion(bf16[8,4,24,512]{3,2,0,1:T(8,128)(2,1)S(1)} %fusion.22, bf16[4,512,3584]{2,1,0:T(8,128)(2,1)} %param.23), kind=kOutput, calls=%fused_computation.25 | convolution fusion | flops 2821324800 | bytes 20971520 | tf_op jit(solution)/shard_map/sexf,efd->sexd/dot_general | solution.py:116
  267.7 3.0 copy.54
  270.7 4.7 %all-to-all-start.1 = ((bf16[32,24,3584]{2,1,0:T(8,128)(2,1)}), bf16[32,24,3584]{2,1,0:T(8,128)(2,1)}, u32[]{:S(2)}, u32[]{:S(2)}) async-start(bf16[32,24,3584]{2,1,0:T(8,128)(2,1)} %bitcast.103), calls=%async_computation.2 | async-start | bytes 11010048 | tf_op jit(solution)/shard_map/all_to_all | solution.py:120
  275.4 0.3 reduce-scatter.5.cloned.1.call-start
  275.7 0.1 copy.55
  275.8 0.1 mul.163
  275.9 0.1 copy.50
  276.0 0.3 fusion.34
  276.3 0.1 copy.56
  276.4 121.1 %all-to-all-done.1 = bf16[32,24,3584]{2,1,0:T(8,128)(2,1)} async-done(((bf16[32,24,3584]{2,1,0:T(8,128)(2,1)}), bf16[32,24,3584]{2,1,0:T(8,128)(2,1)}, u32[]{:S(2)}, u32[]{:S(2)}) %all-to-all-start.1) | async-done | bytes 5505056 | tf_op jit(solution)/shard_map/all_to_all | solution.py:120
  397.5 11.3 %gather_fusion = bf16[512,3584]{1,0:T(8,128)(2,1)} fusion(bf16[768,3584]{1,0:T(8,128)(2,1)} %bitcast.18, s32[1024]{0:T(1024)S(1)} %pad_clamp_fusion), kind=kCustom, calls=%fused_computation | custom fusion | bytes 7342080 | tf_op jit(solution)/shard_map/jit(_take)/gather | solution.py:123
  408.8 6.8 %multiply_reduce_fusion = bf16[64,3584]{1,0:T(8,128)(2,1)} fusion(bf16[512,3584]{1,0:T(8,128)(2,1)} %gather_fusion, f32[64,8]{1,0:T(8,128)S(1)} %copy.56, pred[64,8]{1,0:T(8,128)(4,1)S(1)} %copy.50), kind=kLoop, calls=%fused_computation.22 | loop fusion | flops 7110656 | bytes 4131328 | tf_op jit(solution)/shard_map/reduce_sum | solution.py:127
  415.6 23.0 %reduce-scatter.5.cloned.1.call-done = bf16[16,3584]{1,0:T(8,128)(2,1)} async-done(((bf16[64,3584]{1,0:T(8,128)(2,1)}), bf16[16,3584]{1,0:T(8,128)(2,1)}) %reduce-scatter.5.cloned.1.call-update) | async-done | bytes 114704 | tf_op jit(solution)/shard_map/reduce_scatter | solution.py:128
  438.5 1.6 add_convert_fusion
  (50 shorter events, 0.5 us)
Async XLA Ops:
  6.5 269.5 %copy-start = (bf16[3584,32]{0,1:T(8,128)(2,1)S(1)}, bf16[3584,32]{0,1:T(8,128)(2,1)}, u32[]{:S(2)}) copy-start(bf16[3584,32]{0,1:T(8,128)(2,1)} %param.19) | copy-start | bytes 688132
  6.5 99.4 %reduce-scatter.3.cloned.1.call-start = ((), (), s32[]{:S(2)}) async-start(), calls=%async_computation.4 | async-start | bytes 1032192 | tf_op jit(solution)/shard_map/reduce_scatter | solution.py:76
  11.6 18.0 %collective-permute-start = (bf16[128,8,192]{0,2,1:T(8,128)(2,1)S(1)}, bf16[128,8,192]{0,2,1:T(8,128)(2,1)S(1)}, u32[]{:S(2)}, u32[]{:S(2)}) collective-permute-start(bf16[128,8,192]{0,2,1:T(8,128)(2,1)S(1)} %get-tuple-element.417), channel_id=1, source_target_pairs={{8,0},{16,8},{24,16},{0,24},{9,1},{17,9},{25,17},{1,25},{10,2},{18... | collective-permute-start | bytes 1179656 | tf_op jit(solution)/shard_map/while/body/eval_jaxpr/ppermute | solution.py:14
  15.6 14.0 %collective-permute-start.1 = (bf16[128,8,128]{2,0,1:T(8,128)(2,1)S(1)}, bf16[128,8,128]{2,0,1:T(8,128)(2,1)S(1)}, u32[]{:S(2)}, u32[]{:S(2)}) collective-permute-start(bf16[128,8,128]{2,0,1:T(8,128)(2,1)S(1)} %get-tuple-element.418), channel_id=1, source_target_pairs={{8,0},{16,8},{24,16},{0,24},{9,1},{17,9},{25,17},{1,25},{10,2},{18... | collective-permute-start | bytes 786440 | tf_op jit(solution)/shard_map/while/body/eval_jaxpr/ppermute | solution.py:14
  30.9 16.6 %collective-permute-start = (bf16[128,8,192]{0,2,1:T(8,128)(2,1)S(1)}, bf16[128,8,192]{0,2,1:T(8,128)(2,1)S(1)}, u32[]{:S(2)}, u32[]{:S(2)}) collective-permute-start(bf16[128,8,192]{0,2,1:T(8,128)(2,1)S(1)} %get-tuple-element.417), channel_id=1, source_target_pairs={{8,0},{16,8},{24,16},{0,24},{9,1},{17,9},{25,17},{1,25},{10,2},{18... | collective-permute-start | bytes 1179656 | tf_op jit(solution)/shard_map/while/body/eval_jaxpr/ppermute | solution.py:14
  34.4 13.1 %collective-permute-start.1 = (bf16[128,8,128]{2,0,1:T(8,128)(2,1)S(1)}, bf16[128,8,128]{2,0,1:T(8,128)(2,1)S(1)}, u32[]{:S(2)}, u32[]{:S(2)}) collective-permute-start(bf16[128,8,128]{2,0,1:T(8,128)(2,1)S(1)} %get-tuple-element.418), channel_id=1, source_target_pairs={{8,0},{16,8},{24,16},{0,24},{9,1},{17,9},{25,17},{1,25},{10,2},{18... | collective-permute-start | bytes 786440 | tf_op jit(solution)/shard_map/while/body/eval_jaxpr/ppermute | solution.py:14
  48.8 15.7 %collective-permute-start = (bf16[128,8,192]{0,2,1:T(8,128)(2,1)S(1)}, bf16[128,8,192]{0,2,1:T(8,128)(2,1)S(1)}, u32[]{:S(2)}, u32[]{:S(2)}) collective-permute-start(bf16[128,8,192]{0,2,1:T(8,128)(2,1)S(1)} %get-tuple-element.417), channel_id=1, source_target_pairs={{8,0},{16,8},{24,16},{0,24},{9,1},{17,9},{25,17},{1,25},{10,2},{18... | collective-permute-start | bytes 1179656 | tf_op jit(solution)/shard_map/while/body/eval_jaxpr/ppermute | solution.py:14
  52.3 12.3 %collective-permute-start.1 = (bf16[128,8,128]{2,0,1:T(8,128)(2,1)S(1)}, bf16[128,8,128]{2,0,1:T(8,128)(2,1)S(1)}, u32[]{:S(2)}, u32[]{:S(2)}) collective-permute-start(bf16[128,8,128]{2,0,1:T(8,128)(2,1)S(1)} %get-tuple-element.418), channel_id=1, source_target_pairs={{8,0},{16,8},{24,16},{0,24},{9,1},{17,9},{25,17},{1,25},{10,2},{18... | collective-permute-start | bytes 786440 | tf_op jit(solution)/shard_map/while/body/eval_jaxpr/ppermute | solution.py:14
  66.2 5.3 %copy-start.3 = (s32[1,4,16,8]{2,3,1,0:T(8,128)S(1)}, s32[1,4,16,8]{2,3,1,0:T(8,128)}, u32[]{:S(2)}) copy-start(s32[1,4,16,8]{2,3,1,0:T(8,128)} %param.20) | copy-start | bytes 6148
  66.2 39.8 %copy-start.1 = (bf16[16,3584]{1,0:T(8,128)(2,1)S(1)}, bf16[16,3584]{1,0:T(8,128)(2,1)}, u32[]{:S(2)}) copy-start(bf16[16,3584]{1,0:T(8,128)(2,1)} %param.17) | copy-start | bytes 344068
  66.2 40.8 %copy-start.4 = (f32[3584]{0:T(1024)S(1)}, f32[3584]{0:T(1024)}, u32[]{:S(2)}) copy-start(f32[3584]{0:T(1024)} %param.18) | copy-start | bytes 43012
  270.7 126.7 %all-to-all-start.1 = ((bf16[32,24,3584]{2,1,0:T(8,128)(2,1)}), bf16[32,24,3584]{2,1,0:T(8,128)(2,1)}, u32[]{:S(2)}, u32[]{:S(2)}) async-start(bf16[32,24,3584]{2,1,0:T(8,128)(2,1)} %bitcast.103), calls=%async_computation.2 | async-start | bytes 11010048 | tf_op jit(solution)/shard_map/all_to_all | solution.py:120
  275.4 163.1 %reduce-scatter.5.cloned.1.call-start = ((), (), s32[]{:S(2)}) async-start(), calls=%async_computation.5 | async-start | bytes 573440 | tf_op jit(solution)/shard_map/reduce_scatter | solution.py:128
  397.5 41.1 %copy-start.2 = (bf16[16,3584]{1,0:T(8,128)(2,1)S(1)}, bf16[16,3584]{1,0:T(8,128)(2,1)}, u32[]{:S(2)}) copy-start(bf16[16,3584]{1,0:T(8,128)(2,1)} %reduce-scatter.3.cloned.1.call-done) | copy-start | bytes 344068
Sparse Core Ops, SparseCore 0:
  71.6 34.3 reduce-scatter.2
  415.7 22.7 reduce-scatter.4
where the time goes:
time: 447 us
  waiting for transfers between devices  214 us (48%)
  blocking collectives  134 us (30%)
  matrix products  35.1 us (8%)
  local copies, waits for them, and re-layouts  19.6 us (4%)
  starting transfers between devices  16.4 us (4%)
  between operations  13.7 us (3%)
  other arithmetic  13.3 us (3%)
    all_to_all x1, blocking collectives, body(): lax.all_to_all(outgoing, 'exp', split_axis=0, concat_axis=0, tiled=True)  125 us
    all_to_all x1, waiting for transfers between devices, body(): lax.all_to_all(partial_value, 'exp', split_axis=0, concat_axis=0, tiled=T...  121 us
    ppermute x6, waiting for transfers between devices, from_behind(): return lax.ppermute(block, axis, route)  38.4 us
    reduce_scatter x1, waiting for transfers between devices, body(): lax.psum_scatter(jnp.dot(attended, w_out, preferred_element_type=jnp.floa...  31.8 us
    reduce_scatter x1, waiting for transfers between devices, body(): lax.psum_scatter(combined.astype(jnp.bfloat16), 'ctx', scatter_dimension=...  23 us
    ppermute x6, starting transfers between devices, from_behind(): return lax.ppermute(block, axis, route)  11.5 us
    gather x1, local copies, waits for them, and re-layouts, body(): jnp.take(flat_back, target, axis=0).reshape(group_rows, top_count, d_model)  11.3 us
    all_gather x1, blocking collectives, body(): column = lax.all_gather(normed, 'ctx', axis=0, tiled=True)  9.75 us
  transfers between devices with their start and end apart: 9, of which 6 were waited for; matrix products, arithmetic and copies ran while one was open for 1% of the time, Pallas kernels for 0%

commit v1 on v0

--- a/solution.py
+++ b/solution.py
@@ -117,7 +117,21 @@
         "sexf,efd->sexd", expert_hidden, w_down, preferred_element_type=jnp.float32
     ).astype(jnp.bfloat16)
     partial_value = partial_value.reshape(sources * local_experts, slots_here, d_model)
-    returned = lax.all_to_all(partial_value, "exp", split_axis=0, concat_axis=0, tiled=True)
+    all_values = lax.axis_size("exp")
+    back = lax.axis_index("exp")
+    high, val2 = (all_values, back)
+    passed = partial_value.shape[0] // high
+    finding = list(partial_value.shape)
+    finding[0] = passed
+    low = finding[0]
+    finding[0] = low * high
+    returned = jnp.zeros(finding, partial_value.dtype)
+    for u in range(high):
+        y1 = lax.dynamic_slice_in_dim(partial_value, (val2 ^ u) * passed, passed, axis=0)
+        if u:
+            tall = tuple(((c, c ^ u) for c in range(high)))
+            y1 = lax.ppermute(y1, "exp", tall)
+        returned = lax.dynamic_update_slice_in_dim(returned, y1, (val2 ^ u) * low, axis=0)
     flat_back = returned.reshape(experts * capacity, d_model)
     picked = (
         jnp.take(flat_back, target, axis=0)

time: 447 us -> 459 us (1.027)
  blocking collectives: 134 us -> 9.75 us
  waiting for transfers between devices: 214 us -> 328 us
  local copies, waits for them, and re-layouts: 19.6 us -> 29 us
  matrix products: 35.1 us -> 41 us
  starting transfers between devices: 16.4 us -> 22 us
    all_to_all x1 -> x0, blocking collectives: 125 us -> none  [body(): lax.all_to_all(outgoing, 'exp', split_axis=0, concat_axis=0, tiled=True)]
    ppermute x0 -> x7, waiting for transfers between devices: none -> 114 us  [body(): y1 = lax.ppermute(y1, 'exp', tall)]
    dynamic_update_slice x0 -> x7, local copies, waits for them, and re-layouts: none -> 6.35 us  [body(): lax.dynamic_update_slice_in_dim(returned, y1, (val2 ^ u) * low, axis=0)]
    ppermute x0 -> x7, starting transfers between devices: none -> 5.63 us  [body(): y1 = lax.ppermute(y1, 'exp', tall)]
  transfers between devices with their start and end apart: 9 -> 16, of which waited for: 6 -> 9; matrix products, arithmetic and copies ran while one was open for 1% -> 2% of each run, Pallas kernels for 0% -> 0%
where the time goes in v1:
time: 459 us; the launch traced here: 458 us
  waiting for transfers between devices  328 us (71%)
  matrix products  41 us (9%)
  local copies, waits for them, and re-layouts  29 us (6%)
  starting transfers between devices  22 us (5%)
  other arithmetic  13.9 us (3%)
  between operations  13.7 us (3%)
  blocking collectives  9.75 us (2%)
    all_to_all x1, waiting for transfers between devices, body(): lax.all_to_all(outgoing, 'exp', split_axis=0, concat_axis=0, tiled=True)  121 us
    ppermute x7, waiting for transfers between devices, body(): y1 = lax.ppermute(y1, 'exp', tall)  114 us
    ppermute x6, waiting for transfers between devices, from_behind(): return lax.ppermute(block, axis, route)  38.4 us
    reduce_scatter x1, waiting for transfers between devices, body(): lax.psum_scatter(jnp.dot(attended, w_out, preferred_element_type=jnp.floa...  31.8 us
    reduce_scatter x1, waiting for transfers between devices, body(): lax.psum_scatter(combined.astype(jnp.bfloat16), 'ctx', scatter_dimension=...  23.1 us
    gather x1, local copies, waits for them, and re-layouts, body(): jnp.take(flat_back, target, axis=0).reshape(group_rows, top_count, d_model)  11.5 us
    ppermute x6, starting transfers between devices, from_behind(): return lax.ppermute(block, axis, route)  11.5 us
    dot_general x1, matrix products, body(): jnp.einsum('sexd,edf->sexf', inputs, w_up, preferred_element_type=jnp.flo...  10.1 us
  transfers between devices with their start and end apart: 16, of which 9 were waited for; matrix products, arithmetic and copies ran while one was open for 2% of the time, Pallas kernels for 0%

profile of v1, /device:TPU:0, one launch (start us, length us, event | category | flops | bytes accessed | tf_op | source)
XLA Modules:
  0.0 458.0 jit_solution(1757959039037953673)
XLA Ops:
  6.6 1.1 copy.40
  7.8 0.2 copy.43
  8.0 1.2 copy.38
  9.2 1.2 copy.39
  10.4 0.4 fusion.46
  10.8 0.1 fusion.35
  10.9 0.6 convolution_add_fusion.1
  11.6 54.3 %while.25 = (s32[]{:T(128)}, f32[8,128]{1,0:T(8,128)S(1)}, f32[8,128]{1,0:T(8,128)S(1)}, f32[8,128,128]{2,1,0:T(8,128)S(1)}, bf16[128,8,192]{0,2,1:T(8,128)(2,1)...) while((s32[]{:T(128)}, f32[8,128]{1,0:T(8,128)S(1)}, ...), condition=%wide.region_5.6_spmd.clone.clone, body=%wide.region_2.5_spmd.clone.clone.sunk | while | flops 252987664 | bytes 7735662 | solution.py:72
  11.6 4.0 collective-permute-start
  15.6 0.5 collective-permute-start.1
  16.2 13.4 %collective-permute-done.1 = bf16[128,8,128]{2,0,1:T(8,128)(2,1)S(1)} collective-permute-done((bf16[128,8,128]{2,0,1:T(8,128)(2,1)S(1)}, bf16[128,8,128]{2,0,1:T(8,128)(2,1)S(1)}, u32[]{:S(2)}, u32[]{:S(2)}) %collective-permute-start.1) | collective-permute-done | bytes 262176 | tf_op jit(solution)/shard_map/while/body/eval_jaxpr/ppermute | solution.py:14
  29.6 0.4 fusion.68
  30.0 0.1 fusion.69
  30.1 0.8 convolution_add_fusion.3
  30.9 3.4 collective-permute-start
  34.5 13.0 %collective-permute-done.1 = bf16[128,8,128]{2,0,1:T(8,128)(2,1)S(1)} collective-permute-done((bf16[128,8,128]{2,0,1:T(8,128)(2,1)S(1)}, bf16[128,8,128]{2,0,1:T(8,128)(2,1)S(1)}, u32[]{:S(2)}, u32[]{:S(2)}) %collective-permute-start.1) | collective-permute-done | bytes 262176 | tf_op jit(solution)/shard_map/while/body/eval_jaxpr/ppermute | solution.py:14
  47.5 0.4 fusion.68
  47.9 0.1 fusion.69
  48.1 0.8 convolution_add_fusion.3
  48.8 3.4 collective-permute-start
  52.4 12.1 %collective-permute-done.1 = bf16[128,8,128]{2,0,1:T(8,128)(2,1)S(1)} collective-permute-done((bf16[128,8,128]{2,0,1:T(8,128)(2,1)S(1)}, bf16[128,8,128]{2,0,1:T(8,128)(2,1)S(1)}, u32[]{:S(2)}, u32[]{:S(2)}) %collective-permute-start.1) | collective-permute-done | bytes 262176 | tf_op jit(solution)/shard_map/while/body/eval_jaxpr/ppermute | solution.py:14
  64.6 0.4 fusion.68
  65.0 0.1 fusion.69
  65.1 0.8 convolution_add_fusion.3
  65.9 0.2 copy.44
  66.2 5.2 %convolution_convert_fusion.1 = bf16[128,3584]{1,0:T(8,128)(2,1)} fusion(bf16[128,1024]{0,1:T(8,128)(2,1)S(1)} %bitcast.108, bf16[1024,3584]{1,0:T(8,128)(2,1)} %param.16), kind=kOutput, calls=%fused_computation.28 | convolution fusion | flops 939982848 | bytes 8519680 | tf_op jit(solution)/shard_map/dot_general | solution.py:77
  71.8 1.2 reduce-window.6
  73.0 0.2 slice_reduce_fusion
  73.2 0.1 fusion.41
  73.6 0.5 fusion.26
  74.2 31.8 %reduce-scatter.3.cloned.1.call-done = bf16[16,3584]{1,0:T(8,128)(2,1)} async-done(((bf16[128,3584]{1,0:T(8,128)(2,1)}), bf16[16,3584]{1,0:T(8,128)(2,1)}) %reduce-scatter.3.cloned.1.call-update) | async-done | bytes 114704 | tf_op jit(solution)/shard_map/reduce_scatter | solution.py:76
  106.0 1.0 multiply_reduce_fusion.1
  107.0 1.0 multiply_convert_fusion
  108.0 9.8 %all_gather.3 = bf16[64,3584]{1,0:T(8,128)(2,1)S(1)} all-gather(bf16[16,3584]{1,0:T(8,128)(2,1)S(1)} %multiply_convert_fusion), channel_id=1, replica_groups=mesh['ctx'=4,'exp'=8] {'ctx'}, dimensions={0}, use_global_device_ids=true | all-gather | bytes 573440 | tf_op jit(solution)/shard_map/all_gather | solution.py:85
  117.8 4.1 convolution_convert_fusion
  121.9 4.7 %all-to-all-start = ((bf16[32,24,3584]{2,1,0:T(8,128)(2,1)}), bf16[32,24,3584]{2,1,0:T(8,128)(2,1)}, u32[]{:S(2)}, u32[]{:S(2)}) async-start(bf16[32,24,3584]{2,1,0:T(8,128)(2,1)} %bitcast.102), calls=%async_computation.1 | async-start | bytes 11010048 | tf_op jit(solution)/shard_map/all_to_all | solution.py:108
  126.6 0.2 reduce-scatter.5.cloned.1.call-start
  127.0 0.7 copy.50
  127.7 120.9 %all-to-all-done = bf16[32,24,3584]{2,1,0:T(8,128)(2,1)} async-done(((bf16[32,24,3584]{2,1,0:T(8,128)(2,1)}), bf16[32,24,3584]{2,1,0:T(8,128)(2,1)}, u32[]{:S(2)}, u32[]{:S(2)}) %all-to-all-start) | async-done | bytes 5505056 | tf_op jit(solution)/shard_map/all_to_all | solution.py:108
  248.6 8.8 %fusion.12 = f32[4,8,24,512]{3,2,1,0:T(8,128)S(1)} fusion(bf16[4,3584,512]{2,1,0:T(8,128)(2,1)} %param.21, bf16[8,4,24,3584]{3,2,1,0:T(8,128)(2,1)} %bitcast.7), kind=kOutput, calls=%fused_computation.20 | convolution fusion | flops 2818572288 | bytes 21757952 | tf_op jit(solution)/shard_map/sexd,edf->sexf/dot_general | solution.py:113
  257.4 10.1 %fusion.22 = bf16[8,4,24,512]{3,2,0,1:T(8,128)(2,1)S(1)} fusion(f32[4,8,24,512]{3,2,1,0:T(8,128)S(1)} %fusion.12, bf16[4,3584,512]{2,1,0:T(8,128)(2,1)} %param.22, bf16[8,4,24,3584]{3,2,1,0:T(8,128)(2,1)} %bitcast.7), kind=kOutput, calls=%fused_computation.31 | convolution fusion | flops 2820931584 | bytes 22544384 | tf_op jit(solution)/shard_map/sexd,edf->sexf/dot_general | solution.py:114
  267.5 8.2 %fusion.17 = bf16[8,4,24,3584]{3,2,0,1:T(8,128)(2,1)S(1)} fusion(bf16[8,4,24,512]{3,2,0,1:T(8,128)(2,1)S(1)} %fusion.22, bf16[4,512,3584]{2,1,0:T(8,128)(2,1)} %param.23), kind=kOutput, calls=%fused_computation.25 | convolution fusion | flops 2821324800 | bytes 20971520 | tf_op jit(solution)/shard_map/sexf,efd->sexd/dot_general | solution.py:116
  275.8 0.5 copy.54
  276.3 2.7 broadcast_in_dim.127
  279.0 2.0 constant_dynamic-slice_fusion
  281.0 0.6 pad_clamp_fusion
  281.6 0.3 fusion.34
  282.1 1.5 collective-permute-start.8
  283.6 2.5 collective-permute-start.7
  286.1 1.6 collective-permute-start.4
  287.7 0.9 constant_dynamic-update-slice_fusion.6
  288.6 41.4 %collective-permute-done.3 = bf16[4,24,3584]{2,1,0:T(8,128)(2,1)S(1)} collective-permute-done((bf16[4,24,3584]{2,1,0:T(8,128)(2,1)}, bf16[4,24,3584]{2,1,0:T(8,128)(2,1)S(1)}, u32[]{:S(2)}, u32[]{:S(2)}) %collective-permute-start.3) | collective-permute-done | bytes 688160 | tf_op jit(solution)/shard_map/ppermute | solution.py:133
  330.0 0.9 constant_dynamic-update-slice_fusion.5
  331.0 26.2 %collective-permute-done.4 = bf16[4,24,3584]{2,1,0:T(8,128)(2,1)S(1)} collective-permute-done((bf16[4,24,3584]{2,1,0:T(8,128)(2,1)}, bf16[4,24,3584]{2,1,0:T(8,128)(2,1)S(1)}, u32[]{:S(2)}, u32[]{:S(2)}) %collective-permute-start.4) | collective-permute-done | bytes 688160 | tf_op jit(solution)/shard_map/ppermute | solution.py:133
  357.2 0.9 constant_dynamic-update-slice_fusion.4
  358.1 46.5 %collective-permute-done.5 = bf16[4,24,3584]{2,1,0:T(8,128)(2,1)S(1)} collective-permute-done((bf16[4,24,3584]{2,1,0:T(8,128)(2,1)}, bf16[4,24,3584]{2,1,0:T(8,128)(2,1)S(1)}, u32[]{:S(2)}, u32[]{:S(2)}) %collective-permute-start.5) | collective-permute-done | bytes 688160 | tf_op jit(solution)/shard_map/ppermute | solution.py:133
  404.6 0.9 constant_dynamic-update-slice_fusion.3
  405.5 0.9 constant_dynamic-update-slice_fusion.2
  406.4 0.9 constant_dynamic-update-slice_fusion.1
  407.3 0.9 constant_dynamic-update-slice_fusion
  408.2 11.5 %gather_fusion = bf16[512,3584]{1,0:T(8,128)(2,1)} fusion(bf16[768,3584]{1,0:T(8,128)(2,1)} %bitcast.18, s32[1024]{0:T(1024)S(1)} %copy-done.6), kind=kCustom, calls=%fused_computation | custom fusion | bytes 7342080 | tf_op jit(solution)/shard_map/jit(_take)/gather | solution.py:137
  419.7 6.8 %multiply_reduce_fusion = bf16[64,3584]{1,0:T(8,128)(2,1)} fusion(bf16[512,3584]{1,0:T(8,128)(2,1)} %gather_fusion, f32[64,8]{1,0:T(8,128)S(1)} %copy.56, pred[64,8]{1,0:T(8,128)(4,1)S(1)} %copy-done.4), kind=kLoop, calls=%fused_computation.22 | loop fusion | flops 7110656 | bytes 4131328 | tf_op jit(solution)/shard_map/reduce_sum | solution.py:141
  426.5 23.1 %reduce-scatter.5.cloned.1.call-done = bf16[16,3584]{1,0:T(8,128)(2,1)} async-done(((bf16[64,3584]{1,0:T(8,128)(2,1)}), bf16[16,3584]{1,0:T(8,128)(2,1)}) %reduce-scatter.5.cloned.1.call-update) | async-done | bytes 114704 | tf_op jit(solution)/shard_map/reduce_scatter | solution.py:142
  449.6 1.6 add_convert_fusion
  (76 shorter events, 1.9 us)
Async XLA Ops:
  6.5 275.1 %copy-start = (bf16[3584,32]{0,1:T(8,128)(2,1)S(1)}, bf16[3584,32]{0,1:T(8,128)(2,1)}, u32[]{:S(2)}) copy-start(bf16[3584,32]{0,1:T(8,128)(2,1)} %param.19) | copy-start | bytes 688132
  6.5 99.4 %reduce-scatter.3.cloned.1.call-start = ((), (), s32[]{:S(2)}) async-start(), calls=%async_computation.3 | async-start | bytes 1032192 | tf_op jit(solution)/shard_map/reduce_scatter | solution.py:76
  11.6 18.0 %collective-permute-start = (bf16[128,8,192]{0,2,1:T(8,128)(2,1)S(1)}, bf16[128,8,192]{0,2,1:T(8,128)(2,1)S(1)}, u32[]{:S(2)}, u32[]{:S(2)}) collective-permute-start(bf16[128,8,192]{0,2,1:T(8,128)(2,1)S(1)} %get-tuple-element.425), channel_id=1, source_target_pairs={{8,0},{16,8},{24,16},{0,24},{9,1},{17,9},{25,17},{1,25},{10,2},{18... | collective-permute-start | bytes 1179656 | tf_op jit(solution)/shard_map/while/body/eval_jaxpr/ppermute | solution.py:14
  15.6 14.0 %collective-permute-start.1 = (bf16[128,8,128]{2,0,1:T(8,128)(2,1)S(1)}, bf16[128,8,128]{2,0,1:T(8,128)(2,1)S(1)}, u32[]{:S(2)}, u32[]{:S(2)}) collective-permute-start(bf16[128,8,128]{2,0,1:T(8,128)(2,1)S(1)} %get-tuple-element.426), channel_id=1, source_target_pairs={{8,0},{16,8},{24,16},{0,24},{9,1},{17,9},{25,17},{1,25},{10,2},{18... | collective-permute-start | bytes 786440 | tf_op jit(solution)/shard_map/while/body/eval_jaxpr/ppermute | solution.py:14
  30.9 16.6 %collective-permute-start = (bf16[128,8,192]{0,2,1:T(8,128)(2,1)S(1)}, bf16[128,8,192]{0,2,1:T(8,128)(2,1)S(1)}, u32[]{:S(2)}, u32[]{:S(2)}) collective-permute-start(bf16[128,8,192]{0,2,1:T(8,128)(2,1)S(1)} %get-tuple-element.425), channel_id=1, source_target_pairs={{8,0},{16,8},{24,16},{0,24},{9,1},{17,9},{25,17},{1,25},{10,2},{18... | collective-permute-start | bytes 1179656 | tf_op jit(solution)/shard_map/while/body/eval_jaxpr/ppermute | solution.py:14
  34.4 13.1 %collective-permute-start.1 = (bf16[128,8,128]{2,0,1:T(8,128)(2,1)S(1)}, bf16[128,8,128]{2,0,1:T(8,128)(2,1)S(1)}, u32[]{:S(2)}, u32[]{:S(2)}) collective-permute-start(bf16[128,8,128]{2,0,1:T(8,128)(2,1)S(1)} %get-tuple-element.426), channel_id=1, source_target_pairs={{8,0},{16,8},{24,16},{0,24},{9,1},{17,9},{25,17},{1,25},{10,2},{18... | collective-permute-start | bytes 786440 | tf_op jit(solution)/shard_map/while/body/eval_jaxpr/ppermute | solution.py:14
  48.8 15.7 %collective-permute-start = (bf16[128,8,192]{0,2,1:T(8,128)(2,1)S(1)}, bf16[128,8,192]{0,2,1:T(8,128)(2,1)S(1)}, u32[]{:S(2)}, u32[]{:S(2)}) collective-permute-start(bf16[128,8,192]{0,2,1:T(8,128)(2,1)S(1)} %get-tuple-element.425), channel_id=1, source_target_pairs={{8,0},{16,8},{24,16},{0,24},{9,1},{17,9},{25,17},{1,25},{10,2},{18... | collective-permute-start | bytes 1179656 | tf_op jit(solution)/shard_map/while/body/eval_jaxpr/ppermute | solution.py:14
  52.3 12.3 %collective-permute-start.1 = (bf16[128,8,128]{2,0,1:T(8,128)(2,1)S(1)}, bf16[128,8,128]{2,0,1:T(8,128)(2,1)S(1)}, u32[]{:S(2)}, u32[]{:S(2)}) collective-permute-start(bf16[128,8,128]{2,0,1:T(8,128)(2,1)S(1)} %get-tuple-element.426), channel_id=1, source_target_pairs={{8,0},{16,8},{24,16},{0,24},{9,1},{17,9},{25,17},{1,25},{10,2},{18... | collective-permute-start | bytes 786440 | tf_op jit(solution)/shard_map/while/body/eval_jaxpr/ppermute | solution.py:14
  66.2 5.3 %copy-start.3 = (s32[1,4,16,8]{2,3,1,0:T(8,128)S(1)}, s32[1,4,16,8]{2,3,1,0:T(8,128)}, u32[]{:S(2)}) copy-start(s32[1,4,16,8]{2,3,1,0:T(8,128)} %param.20) | copy-start | bytes 6148
  66.2 39.8 %copy-start.1 = (bf16[16,3584]{1,0:T(8,128)(2,1)S(1)}, bf16[16,3584]{1,0:T(8,128)(2,1)}, u32[]{:S(2)}) copy-start(bf16[16,3584]{1,0:T(8,128)(2,1)} %param.17) | copy-start | bytes 344068
  66.2 40.8 %copy-start.5 = (f32[3584]{0:T(1024)S(1)}, f32[3584]{0:T(1024)}, u32[]{:S(2)}) copy-start(f32[3584]{0:T(1024)} %param.18) | copy-start | bytes 43012
  121.9 126.7 %all-to-all-start = ((bf16[32,24,3584]{2,1,0:T(8,128)(2,1)}), bf16[32,24,3584]{2,1,0:T(8,128)(2,1)}, u32[]{:S(2)}, u32[]{:S(2)}) async-start(bf16[32,24,3584]{2,1,0:T(8,128)(2,1)} %bitcast.102), calls=%async_computation.1 | async-start | bytes 11010048 | tf_op jit(solution)/shard_map/all_to_all | solution.py:108
  126.6 323.1 %reduce-scatter.5.cloned.1.call-start = ((), (), s32[]{:S(2)}) async-start(), calls=%async_computation.4 | async-start | bytes 573440 | tf_op jit(solution)/shard_map/reduce_scatter | solution.py:142
  281.0 5.1 %collective-permute-start.2 = (bf16[4,24,3584]{2,1,0:T(8,128)(2,1)}, bf16[4,24,3584]{2,1,0:T(8,128)(2,1)S(1)}, u32[]{:S(2)}, u32[]{:S(2)}) collective-permute-start(bf16[4,24,3584]{2,1,0:T(8,128)(2,1)} %get-tuple-element.334), channel_id=1, source_target_pairs={{0,1},{1,0},{2,3},{3,2},{4,5},{5,4},{6,7},{7,6},{8,9},{9,8},{10,11... | collective-permute-start | bytes 2064392 | tf_op jit(solution)/shard_map/ppermute | solution.py:133
  281.9 126.3 %copy-start.6 = (s32[1024]{0:T(1024)S(1)}, s32[1024]{0:T(1024)}, u32[]{:S(2)}) copy-start(s32[1024]{0:T(1024)} %pad_clamp_fusion) | copy-start | bytes 12292
  282.0 48.1 %collective-permute-start.3 = (bf16[4,24,3584]{2,1,0:T(8,128)(2,1)}, bf16[4,24,3584]{2,1,0:T(8,128)(2,1)S(1)}, u32[]{:S(2)}, u32[]{:S(2)}) collective-permute-start(bf16[4,24,3584]{2,1,0:T(8,128)(2,1)} %get-tuple-element.333), channel_id=1, source_target_pairs={{0,2},{1,3},{2,0},{3,1},{4,6},{5,7},{6,4},{7,5},{8,10},{9,11},{10,... | collective-permute-start | bytes 2064392 | tf_op jit(solution)/shard_map/ppermute | solution.py:133
  282.1 125.2 %collective-permute-start.8 = (bf16[4,24,3584]{2,1,0:T(8,128)(2,1)S(1)}, bf16[4,24,3584]{2,1,0:T(8,128)(2,1)S(1)}, u32[]{:S(2)}, u32[]{:S(2)}) collective-permute-start(bf16[4,24,3584]{2,1,0:T(8,128)(2,1)S(1)} %get-tuple-element.328), channel_id=1, source_target_pairs={{0,7},{1,6},{2,5},{3,4},{4,3},{5,2},{6,1},{7,0},{8,15},{9,14},{10,... | collective-permute-start | bytes 2064392 | tf_op jit(solution)/shard_map/ppermute | solution.py:133
  283.6 122.8 %collective-permute-start.7 = (bf16[4,24,3584]{2,1,0:T(8,128)(2,1)S(1)}, bf16[4,24,3584]{2,1,0:T(8,128)(2,1)S(1)}, u32[]{:S(2)}, u32[]{:S(2)}) collective-permute-start(bf16[4,24,3584]{2,1,0:T(8,128)(2,1)S(1)} %get-tuple-element.329), channel_id=1, source_target_pairs={{0,6},{1,7},{2,4},{3,5},{4,2},{5,3},{6,0},{7,1},{8,14},{9,15},{10,... | collective-permute-start | bytes 2064392 | tf_op jit(solution)/shard_map/ppermute | solution.py:133
  286.1 119.4 %collective-permute-start.6 = (bf16[4,24,3584]{2,1,0:T(8,128)(2,1)}, bf16[4,24,3584]{2,1,0:T(8,128)(2,1)S(1)}, u32[]{:S(2)}, u32[]{:S(2)}) collective-permute-start(bf16[4,24,3584]{2,1,0:T(8,128)(2,1)} %get-tuple-element.330), channel_id=1, source_target_pairs={{0,5},{1,4},{2,7},{3,6},{4,1},{5,0},{6,3},{7,2},{8,13},{9,12},{10,... | collective-permute-start | bytes 2064392 | tf_op jit(solution)/shard_map/ppermute | solution.py:133
  286.1 71.1 %collective-permute-start.4 = (bf16[4,24,3584]{2,1,0:T(8,128)(2,1)}, bf16[4,24,3584]{2,1,0:T(8,128)(2,1)S(1)}, u32[]{:S(2)}, u32[]{:S(2)}) collective-permute-start(bf16[4,24,3584]{2,1,0:T(8,128)(2,1)} %get-tuple-element.332), channel_id=1, source_target_pairs={{0,3},{1,2},{2,1},{3,0},{4,7},{5,6},{6,5},{7,4},{8,11},{9,10},{10,... | collective-permute-start | bytes 2064392 | tf_op jit(solution)/shard_map/ppermute | solution.py:133
  330.0 74.5 %collective-permute-start.5 = (bf16[4,24,3584]{2,1,0:T(8,128)(2,1)}, bf16[4,24,3584]{2,1,0:T(8,128)(2,1)S(1)}, u32[]{:S(2)}, u32[]{:S(2)}) collective-permute-start(bf16[4,24,3584]{2,1,0:T(8,128)(2,1)} %get-tuple-element.331), channel_id=1, source_target_pairs={{0,4},{1,5},{2,6},{3,7},{4,0},{5,1},{6,2},{7,3},{8,12},{9,13},{10,... | collective-permute-start | bytes 2064392 | tf_op jit(solution)/shard_map/ppermute | solution.py:133
  408.2 11.5 %copy-start.4 = (pred[64,8]{1,0:T(8,128)(4,1)S(1)}, pred[64,8]{1,0:T(8,128)(4,1)}, u32[]{:S(2)}) copy-start(pred[64,8]{1,0:T(8,128)(4,1)} %copy.50) | copy-start | bytes 1540
  408.2 41.4 %copy-start.2 = (bf16[16,3584]{1,0:T(8,128)(2,1)S(1)}, bf16[16,3584]{1,0:T(8,128)(2,1)}, u32[]{:S(2)}) copy-start(bf16[16,3584]{1,0:T(8,128)(2,1)} %reduce-scatter.3.cloned.1.call-done) | copy-start | bytes 344068
Sparse Core Ops, SparseCore 0:
  71.6 34.3 reduce-scatter.2
  426.6 22.9 reduce-scatter.4
